TPU v7x, 256 devices: a whole 4x4x8 slice. The times are simulated.
256 devices in a mesh: section: 8 (over x, core), seq: 32 (over z, y).
Axes of the slice: x: 4, y: 4, z: 8, core: 2. Of those that a mesh axis runs over, the one named last changes fastest.
Arguments:
- queries: bfloat16 [8, 10240, 4096], P('section', 'seq'), may hold values from -60 to 60
- keys_new: bfloat16 [8, 10240, 4096], P('section', 'seq'), may hold values from -6 to 6
- values_new: bfloat16 [8, 10240, 4096], P('section', 'seq'), may hold values from -6 to 6
- keys_cache: bfloat16 [8, 6144, 4096], P('section', None, 'seq'), may hold values from -6 to 6
- values_cache: bfloat16 [8, 6144, 4096], P('section', None, 'seq'), may hold values from -6 to 6
- window: int32 [8, 32], P('section', 'seq'), may hold values from 1 to 3, as said below
- global_blocks: int32 [8, 2], P('section'), may hold values from 0 to 95
- random_blocks: int32 [8, 160, 3], P('section'), may hold values from 0 to 95
Outputs:
- handed: bfloat16 [8, 10240, 4096], P('section', 'seq')
Inputs may be any that keep to these rules, and one draw needn't show every extreme that they name: In every section some head has the window 3.
All inputs are finite; a program needn't handle non-finite values.
Results may differ from a plain program's by a relative error of at most 0.0049.
Values may be sent and summed in bfloat16 or wider, within the bound.
A program may use at most 128 MiB of HBM per device.

v0:
```python
import math
import jax
import jax.numpy as jnp
from jax import lax
from jax.sharding import PartitionSpec as P

HD = 128
BLK = 64
WMAX = 3
GLOB = 2
RAND = 3
NK = 8
masked_score = -1e30


def as_sent(shard):

    def short(part):
        return part.astype(jnp.bfloat16) if part.dtype == jnp.float32 else part

    return jax.tree.map(short, shard)


def passed_along(shard, axis, by):
    devices = lax.axis_size(axis)
    return lax.ppermute(shard, axis, [(i, (i + by) % devices) for i in range(devices)])


def block_mask(span_blocks):
    rows = jnp.arange(BLK, dtype=jnp.int32)[:, None]
    column = jnp.arange(NK * BLK, dtype=jnp.int32)[None, :]
    which = column // BLK
    inside = column % BLK
    allowed = jnp.where(which >= WMAX, True, which < span_blocks)
    return allowed & ((which != 0) | (inside <= rows))


def attend_local(
    query,
    fresh_keys,
    fresh_values,
    old_keys,
    old_values,
    span_blocks,
    global_row,
    random_rows,
    group,
):
    stretch_rows = query.shape[0]
    block_count = stretch_rows // BLK
    cache_blocks = old_keys.shape[0] // BLK
    lead = (WMAX - 1) * BLK
    near_keys = jnp.concatenate([old_keys[old_keys.shape[0] - lead :], fresh_keys], axis=0)
    near_values = jnp.concatenate([old_values[old_values.shape[0] - lead :], fresh_values], axis=0)
    glob_keys = jnp.concatenate(
        [lax.dynamic_slice_in_dim(old_keys, global_row[g] * BLK, BLK, 0) for g in range(GLOB)],
        axis=0,
    )
    glob_values = jnp.concatenate(
        [lax.dynamic_slice_in_dim(old_values, global_row[g] * BLK, BLK, 0) for g in range(GLOB)],
        axis=0,
    )
    key_blocks = old_keys.reshape(cache_blocks, BLK, HD)
    value_blocks = old_values.reshape(cache_blocks, BLK, HD)
    query_blocks = query.reshape(block_count, BLK, HD)
    allowed = block_mask(span_blocks)
    scale = 1.0 / math.sqrt(HD)

    def one_group(index):
        first = index * group
        query_part = lax.dynamic_slice_in_dim(query_blocks, first, group, 0)
        near_key_part = lax.dynamic_slice_in_dim(
            near_keys, first * BLK, (group + WMAX - 1) * BLK, 0
        )
        near_value_part = lax.dynamic_slice_in_dim(
            near_values, first * BLK, (group + WMAX - 1) * BLK, 0
        )
        random_part = lax.dynamic_slice_in_dim(random_rows, first, group, 0)
        rand_keys = key_blocks[random_part].reshape(group, RAND * BLK, HD)
        rand_values = value_blocks[random_part].reshape(group, RAND * BLK, HD)
        near_value_list = []
        pieces = []
        for slot in range(WMAX):
            offset = (WMAX - 1 - slot) * BLK
            slot_keys = near_key_part[offset : offset + group * BLK].reshape(group, BLK, HD)
            near_value_list.append(
                near_value_part[offset : offset + group * BLK].reshape(group, BLK, HD)
            )
            pieces.append(
                jnp.einsum(
                    "gih,gjh->gij", query_part, slot_keys, preferred_element_type=jnp.float32
                )
            )
        pieces.append(
            jnp.einsum("gih,jh->gij", query_part, glob_keys, preferred_element_type=jnp.float32)
        )
        pieces.append(
            jnp.einsum("gih,gjh->gij", query_part, rand_keys, preferred_element_type=jnp.float32)
        )
        scores = jnp.concatenate(pieces, axis=2) * scale
        scores = jnp.where(allowed[None], scores, masked_score)
        top = jnp.max(scores, axis=-1, keepdims=True)
        expo = jnp.exp(scores - top)
        weights = (expo / jnp.sum(expo, axis=-1, keepdims=True)).astype(jnp.bfloat16)
        result = jnp.einsum(
            "gij,gjh->gih",
            weights[:, :, WMAX * BLK + GLOB * BLK :],
            rand_values,
            preferred_element_type=jnp.float32,
        )
        result = result + jnp.einsum(
            "gij,jh->gih",
            weights[:, :, WMAX * BLK : WMAX * BLK + GLOB * BLK],
            glob_values,
            preferred_element_type=jnp.float32,
        )
        for slot in range(WMAX):
            result = result + jnp.einsum(
                "gij,gjh->gih",
                weights[:, :, slot * BLK : (slot + 1) * BLK],
                near_value_list[slot],
                preferred_element_type=jnp.float32,
            )
        return result.astype(jnp.bfloat16)

    outputs = lax.map(one_group, jnp.arange(block_count // group, dtype=jnp.int32))
    return outputs.reshape(stretch_rows, HD)


def per_device(
    queries, keys_new, values_new, keys_cache, values_cache, window, global_blocks, random_blocks
):
    head_queries = lax.all_to_all(queries, "seq", split_axis=2, concat_axis=1, tiled=True)
    head_keys, head_values = (
        lax.all_to_all(keys_new, "seq", split_axis=2, concat_axis=1, tiled=True),
        lax.all_to_all(values_new, "seq", split_axis=2, concat_axis=1, tiled=True),
    )
    stretch_rows = head_queries.shape[1]
    block_count = stretch_rows // BLK
    group = math.gcd(block_count, 8)
    global_row = global_blocks[0]
    random_rows = random_blocks[0]
    results = [
        attend_local(
            head_queries[0],
            head_keys[0],
            head_values[0],
            keys_cache[0],
            values_cache[0],
            window[0, 0],
            global_row,
            random_rows,
            group,
        )
    ]
    attended = jnp.concatenate(results, axis=1)[None]
    regrouped = lax.all_to_all(
        as_sent(attended), "seq", split_axis=1, concat_axis=2, tiled=True
    ).astype(attended.dtype)
    return passed_along(as_sent(regrouped), "section", 1).astype(regrouped.dtype)


def solution(mesh):
    placed = (
        P("section", "seq", None),
        P("section", "seq", None),
        P("section", "seq", None),
        P("section", None, "seq"),
        P("section", None, "seq"),
        P("section", "seq"),
        P("section", None),
        P("section", None, None),
    )
    return jax.shard_map(
        per_device, mesh=mesh, in_specs=placed, out_specs=P("section", "seq", None), check_vma=False
    )
```

profile of v0, /device:TPU:32, one launch (start us, length us, event | category | flops | bytes accessed | tf_op | source)
XLA Modules:
  0.0 889.0 jit_solution(13821503862325278436)
XLA Ops:
  0.0 14.3 %copy.46 = bf16[1,320,4096]{1,0,2:T(2,128)(2,1)} copy(bf16[1,320,4096]{2,1,0:T(8,128)(2,1)} %param.12) | data formatting | bytes 5242880 | tf_op args[2]
  14.9 67.0 %reduce.2 = bf16[4096,320]{1,0:T(8,128)(2,1)S(1)} reduce(bf16[4096,1,320]{2,1,0:T(2,128)(2,1)} %bitcast.118, bf16[]{:T(256)} %broadcast.139), dimensions={1}, to_apply=%bitcast.58.reduce_sub_computation | reduce | bytes 5242882
  81.9 4.4 reshape.177
  86.3 12.1 %all-to-all-start.2 = ((bf16[32,2,20480]{2,1,0:T(2,128)(2,1)}), bf16[32,2,20480]{2,1,0:T(2,128)(2,1)}, u32[]{:S(2)}, u32[]{:S(2)}) async-start(bf16[32,2,20480]{2,1,0:T(2,128)(2,1)} %reshape.177), calls=%async_computation.2 | async-start | bytes 5242880 | tf_op jit(solution)/shard_map/all_to_all | solution.py:136
  98.5 12.3 %copy.42 = bf16[1,320,4096]{1,0,2:T(2,128)(2,1)} copy(bf16[1,320,4096]{2,1,0:T(8,128)(2,1)S(1)} %copy-done.2) | data formatting | bytes 5242880 | tf_op args[1]
  110.8 67.0 %reduce.1 = bf16[4096,320]{1,0:T(8,128)(2,1)S(1)} reduce(bf16[4096,1,320]{2,1,0:T(2,128)(2,1)} %bitcast.122, bf16[]{:T(256)} %broadcast.139), dimensions={1}, to_apply=%bitcast.56.reduce_sub_computation | reduce | bytes 5242882
  177.8 4.3 reshape.175
  182.2 10.8 %all-to-all-start.1 = ((bf16[32,2,20480]{2,1,0:T(2,128)(2,1)}), bf16[32,2,20480]{2,1,0:T(2,128)(2,1)}, u32[]{:S(2)}, u32[]{:S(2)}) async-start(bf16[32,2,20480]{2,1,0:T(2,128)(2,1)} %reshape.175), calls=%async_computation.1 | async-start | bytes 5242880 | tf_op jit(solution)/shard_map/all_to_all | solution.py:135
  193.0 12.3 %copy.39 = bf16[1,320,4096]{1,0,2:T(2,128)(2,1)} copy(bf16[1,320,4096]{2,1,0:T(8,128)(2,1)S(1)} %copy-done.3) | data formatting | bytes 5242880 | tf_op args[0]
  205.3 67.0 %reduce = bf16[4096,320]{1,0:T(8,128)(2,1)S(1)} reduce(bf16[4096,1,320]{2,1,0:T(2,128)(2,1)} %bitcast.123, bf16[]{:T(256)} %broadcast.139), dimensions={1}, to_apply=%bitcast.54.reduce_sub_computation | reduce | bytes 5242882
  272.4 4.4 reshape.173
  276.8 10.3 %all-to-all-start = ((bf16[32,2,20480]{2,1,0:T(2,128)(2,1)}), bf16[32,2,20480]{2,1,0:T(2,128)(2,1)}, u32[]{:S(2)}, u32[]{:S(2)}) async-start(bf16[32,2,20480]{2,1,0:T(2,128)(2,1)} %reshape.173), calls=%async_computation | async-start | bytes 5242880 | tf_op jit(solution)/shard_map/all_to_all | solution.py:133
  292.1 19.9 %reshape.178 = bf16[4096,1,320]{2,1,0:T(2,128)(2,1)} reshape(bf16[32,2,20480]{2,1,0:T(2,128)(2,1)} %all-to-all-done.2) | data formatting | bytes 5242880
  318.6 4.2 copy.48
  322.8 19.9 %reshape.176 = bf16[4096,1,320]{2,1,0:T(2,128)(2,1)} reshape(bf16[32,2,20480]{2,1,0:T(2,128)(2,1)} %all-to-all-done.1) | data formatting | bytes 5242880
  349.2 4.3 copy.44
  353.6 19.9 %reshape.174 = bf16[4096,1,320]{2,1,0:T(2,128)(2,1)} reshape(bf16[32,2,20480]{2,1,0:T(2,128)(2,1)} %all-to-all-done) | data formatting | bytes 5242880
  380.1 4.4 copy.41
  387.1 322.0 %while.13 = (s32[]{:T(128)}, bf16[20,8,64,128]{3,2,1,0:T(8,128)(2,1)}, s32[20]{0:T(128)S(1)}, bf16[160,64,128]{2,1,0:T(8,128)(2,1)}, bf16[10368,128]{1,0:T(8,128...) while((s32[]{:T(128)}, ...), condition=%wide.region_3.4_spmd.clone, body=%wide.region_0.3_spmd.clone.sunk | while | flops 136218192 | bytes 15348233 | solution.py:126
  709.1 6.0 copy.62
  715.0 56.2 %reduce.3 = bf16[10240,128]{1,0:T(8,128)(2,1)S(1)} reduce(bf16[10240,1,128]{2,1,0:T(2,128)(2,1)} %bitcast.124, bf16[]{:T(256)} %broadcast.139), dimensions={1}, to_apply=%bitcast.72.reduce_sub_computation | reduce | bytes 5242882
  773.5 70.3 %all_to_all.63 = bf16[32,2,20480]{2,1,0:T(2,128)(2,1)S(1)} all-to-all(bf16[32,2,20480]{2,1,0:T(2,128)(2,1)} %reshape.179), channel_id=1, replica_groups=mesh['section'=8,'seq'=32] {'seq'}, dimensions={0} | all-to-all | bytes 5242880 | tf_op jit(solution)/shard_map/all_to_all | solution.py:157
  843.8 7.2 reshape.180
  855.0 32.3 %collective-permute-done = bf16[1,320,4096]{2,1,0:T(8,128)(2,1)S(1)} collective-permute-done((bf16[1,320,4096]{2,1,0:T(8,128)(2,1)S(1)}, bf16[1,320,4096]{2,1,0:T(8,128)(2,1)S(1)}, u32[]{:S(2)}, u32[]{:S(2)}) %collective-permute-start) | collective-permute-done | bytes 2621472 | tf_op jit(solution)/shard_map/ppermute | solution.py:26
  (459 shorter events, 327.9 us)
Async XLA Ops:
  86.3 12.2 %copy-start.2 = (bf16[1,320,4096]{2,1,0:T(8,128)(2,1)S(1)}, bf16[1,320,4096]{2,1,0:T(8,128)(2,1)}, u32[]{:S(2)}) copy-start(bf16[1,320,4096]{2,1,0:T(8,128)(2,1)} %param.11) | copy-start | bytes 7864324
  86.3 95.9 %all-to-all-start.2 = ((bf16[32,2,20480]{2,1,0:T(2,128)(2,1)}), bf16[32,2,20480]{2,1,0:T(2,128)(2,1)}, u32[]{:S(2)}, u32[]{:S(2)}) async-start(bf16[32,2,20480]{2,1,0:T(2,128)(2,1)} %reshape.177), calls=%async_computation.2 | async-start | bytes 5242880 | tf_op jit(solution)/shard_map/all_to_all | solution.py:136
  182.2 10.8 %copy-start.3 = (bf16[1,320,4096]{2,1,0:T(8,128)(2,1)S(1)}, bf16[1,320,4096]{2,1,0:T(8,128)(2,1)}, u32[]{:S(2)}) copy-start(bf16[1,320,4096]{2,1,0:T(8,128)(2,1)} %param.10) | copy-start | bytes 7864324
  182.2 94.6 %all-to-all-start.1 = ((bf16[32,2,20480]{2,1,0:T(2,128)(2,1)}), bf16[32,2,20480]{2,1,0:T(2,128)(2,1)}, u32[]{:S(2)}, u32[]{:S(2)}) async-start(bf16[32,2,20480]{2,1,0:T(2,128)(2,1)} %reshape.175), calls=%async_computation.1 | async-start | bytes 5242880 | tf_op jit(solution)/shard_map/all_to_all | solution.py:135
  276.8 10.3 %copy-start.5 = (s32[1,2]{1,0:T(1,128)S(1)}, s32[1,2]{1,0:T(1,128)}, u32[]{:S(2)}) copy-start(s32[1,2]{1,0:T(1,128)} %param.16) | copy-start | bytes 28
  276.8 12.9 %copy-start.4 = (s32[1,160,3]{1,0,2:T(1,128)S(1)}, s32[1,160,3]{1,0,2:T(1,128)}, u32[]{:S(2)}) copy-start(s32[1,160,3]{1,0,2:T(1,128)} %param.17) | copy-start | bytes 5764
  276.8 76.8 %all-to-all-start = ((bf16[32,2,20480]{2,1,0:T(2,128)(2,1)}), bf16[32,2,20480]{2,1,0:T(2,128)(2,1)}, u32[]{:S(2)}, u32[]{:S(2)}) async-start(bf16[32,2,20480]{2,1,0:T(2,128)(2,1)} %reshape.173), calls=%async_computation | async-start | bytes 5242880 | tf_op jit(solution)/shard_map/all_to_all | solution.py:133
  380.1 4.4 copy-start
  380.1 4.4 copy-start.1
  855.0 32.3 %collective-permute-start = (bf16[1,320,4096]{2,1,0:T(8,128)(2,1)S(1)}, bf16[1,320,4096]{2,1,0:T(8,128)(2,1)S(1)}, u32[]{:S(2)}, u32[]{:S(2)}) collective-permute-start(bf16[1,320,4096]{2,1,0:T(8,128)(2,1)S(1)} %bitcast.143), channel_id=1, source_target_pairs={{0,32},{32,64},{64,96},{96,128},{128,160},{160,192},{192,224},{224... | collective-permute-start | bytes 7864328 | tf_op jit(solution)/shard_map/ppermute | solution.py:26
where the time goes:
time: 903 us; the launch traced here: 889 us
  local copies, waits for them, and re-layouts  304 us (34%)
  other arithmetic  271 us (30%)
  matrix products  148 us (16%)
  blocking collectives  70.3 us (8%)
  starting transfers between devices  33.3 us (4%)
  waiting for transfers between devices  32.3 us (4%)
  loops' own time  27.7 us (3%)
    unnamed x4, other arithmetic  257 us
    unnamed x30, local copies, waits for them, and re-layouts  137 us
    all_to_all x1, blocking collectives, per_device(): lax.all_to_all(as_sent(attended), 'seq', split_axis=1, concat_axis=2, til...  70.3 us
    dot_general x60, matrix products, one_group(): jnp.einsum('gih,gjh->gij', query_part, slot_keys, preferred_element_type=...  65.6 us
    gather x20, local copies, waits for them, and re-layouts, one_group(): rand_values = value_blocks[random_part].reshape(group, RAND * BLK, HD)  40.6 us
    gather x20, local copies, waits for them, and re-layouts, one_group(): rand_keys = key_blocks[random_part].reshape(group, RAND * BLK, HD)  40.6 us
    ppermute x1, waiting for transfers between devices, passed_along(): lax.ppermute(shard, axis, [(i, (i + by) % devices) for i in range(devices)])  32.3 us
    another operation x1, loops' own time, attend_local(): lax.map(one_group, jnp.arange(block_count // group, dtype=jnp.int32))  27.7 us
  transfers between devices with their start and end apart: 4, of which 1 were waited for; matrix products, arithmetic and copies ran while one was open for 26% of the time, Pallas kernels for 0%

commit v1 on v0

--- a/solution.py
+++ b/solution.py
@@ -11,6 +11,12 @@
 RAND = 3
 NK = 8
 masked_score = -1e30
+
+
+def swap_blocks(x, axis, split, join):
+    pieces = jnp.split(x, lax.axis_size(axis), axis=split)
+    incoming = lax.all_to_all(jnp.stack(pieces), axis, 0, 0)
+    return jnp.concatenate(incoming, axis=join)
 
 
 def as_sent(shard):
@@ -154,9 +160,7 @@
         )
     ]
     attended = jnp.concatenate(results, axis=1)[None]
-    regrouped = lax.all_to_all(
-        as_sent(attended), "seq", split_axis=1, concat_axis=2, tiled=True
-    ).astype(attended.dtype)
+    regrouped = swap_blocks(as_sent(attended), "seq", 1, 2).astype(attended.dtype)
     return passed_along(as_sent(regrouped), "section", 1).astype(regrouped.dtype)
 
 

time: 903 us -> 850 us (0.941)
  other arithmetic: 271 us -> 215 us
    unnamed x4 -> x3, other arithmetic: 257 us -> 201 us
    unnamed x30 -> x58, local copies, waits for them, and re-layouts: 137 us -> 152 us
  transfers between devices with their start and end apart: 4 -> 4, of which waited for: 1 -> 1; matrix products, arithmetic and copies ran while one was open for 26% -> 28% of each run, Pallas kernels for 0% -> 0%
where the time goes in v1:
time: 850 us; the launch traced here: 840 us
  local copies, waits for them, and re-layouts  312 us (37%)
  other arithmetic  215 us (25%)
  matrix products  148 us (17%)
  blocking collectives  70.1 us (8%)
  waiting for transfers between devices  32.3 us (4%)
  starting transfers between devices  31.8 us (4%)
  loops' own time  28.3 us (3%)
    unnamed x3, other arithmetic  201 us
    unnamed x58, local copies, waits for them, and re-layouts  152 us
    all_to_all x1, blocking collectives, swap_blocks(): incoming = lax.all_to_all(jnp.stack(pieces), axis, 0, 0)  70.1 us
    dot_general x60, matrix products, one_group(): jnp.einsum('gih,gjh->gij', query_part, slot_keys, preferred_element_type=...  65.6 us
    gather x20, local copies, waits for them, and re-layouts, one_group(): rand_keys = key_blocks[random_part].reshape(group, RAND * BLK, HD)  40.6 us
    gather x20, local copies, waits for them, and re-layouts, one_group(): rand_values = value_blocks[random_part].reshape(group, RAND * BLK, HD)  40.6 us
    ppermute x1, waiting for transfers between devices, passed_along(): lax.ppermute(shard, axis, [(i, (i + by) % devices) for i in range(devices)])  32.3 us
    another operation x1, loops' own time, attend_local(): lax.map(one_group, jnp.arange(block_count // group, dtype=jnp.int32))  28.3 us
  transfers between devices with their start and end apart: 4, of which 1 were waited for; matrix products, arithmetic and copies ran while one was open for 28% of the time, Pallas kernels for 0%

profile of v1, /device:TPU:32, one launch (start us, length us, event | category | flops | bytes accessed | tf_op | source)
XLA Modules:
  0.0 840.0 jit_solution(10011276780195649076)
XLA Ops:
  0.0 14.3 %copy.76 = bf16[1,320,4096]{1,0,2:T(2,128)(2,1)} copy(bf16[1,320,4096]{2,1,0:T(8,128)(2,1)} %param.12) | data formatting | bytes 5242880 | tf_op args[2]
  14.8 67.0 %reduce.2 = bf16[4096,320]{1,0:T(8,128)(2,1)S(1)} reduce(bf16[4096,1,320]{2,1,0:T(2,128)(2,1)} %bitcast.241, bf16[]{:T(256)} %broadcast.139), dimensions={1}, to_apply=%bitcast.184.reduce_sub_computation | reduce | bytes 5242882
  81.8 4.4 reshape.185
  86.2 11.7 %all-to-all-start.2 = ((bf16[32,2,20480]{2,1,0:T(2,128)(2,1)}), bf16[32,2,20480]{2,1,0:T(2,128)(2,1)}, u32[]{:S(2)}, u32[]{:S(2)}) async-start(bf16[32,2,20480]{2,1,0:T(2,128)(2,1)} %reshape.185), calls=%async_computation.2 | async-start | bytes 5242880 | tf_op jit(solution)/shard_map/all_to_all | solution.py:142
  97.9 12.3 %copy.72 = bf16[1,320,4096]{1,0,2:T(2,128)(2,1)} copy(bf16[1,320,4096]{2,1,0:T(8,128)(2,1)S(1)} %copy-done.2) | data formatting | bytes 5242880 | tf_op args[1]
  110.2 67.0 %reduce.1 = bf16[4096,320]{1,0:T(8,128)(2,1)S(1)} reduce(bf16[4096,1,320]{2,1,0:T(2,128)(2,1)} %bitcast.246, bf16[]{:T(256)} %broadcast.139), dimensions={1}, to_apply=%bitcast.182.reduce_sub_computation | reduce | bytes 5242882
  177.2 4.3 reshape.183
  181.5 10.1 %all-to-all-start.1 = ((bf16[32,2,20480]{2,1,0:T(2,128)(2,1)}), bf16[32,2,20480]{2,1,0:T(2,128)(2,1)}, u32[]{:S(2)}, u32[]{:S(2)}) async-start(bf16[32,2,20480]{2,1,0:T(2,128)(2,1)} %reshape.183), calls=%async_computation.1 | async-start | bytes 5242880 | tf_op jit(solution)/shard_map/all_to_all | solution.py:141
  191.6 12.3 %copy.69 = bf16[1,320,4096]{1,0,2:T(2,128)(2,1)} copy(bf16[1,320,4096]{2,1,0:T(8,128)(2,1)S(1)} %copy-done.3) | data formatting | bytes 5242880 | tf_op args[0]
  204.0 67.0 %reduce = bf16[4096,320]{1,0:T(8,128)(2,1)S(1)} reduce(bf16[4096,1,320]{2,1,0:T(2,128)(2,1)} %bitcast.242, bf16[]{:T(256)} %broadcast.139), dimensions={1}, to_apply=%bitcast.180.reduce_sub_computation | reduce | bytes 5242882
  270.9 4.4 reshape.181
  275.3 10.0 %all-to-all-start = ((bf16[32,2,20480]{2,1,0:T(2,128)(2,1)}), bf16[32,2,20480]{2,1,0:T(2,128)(2,1)}, u32[]{:S(2)}, u32[]{:S(2)}) async-start(bf16[32,2,20480]{2,1,0:T(2,128)(2,1)} %reshape.181), calls=%async_computation | async-start | bytes 5242880 | tf_op jit(solution)/shard_map/all_to_all | solution.py:139
  290.2 19.8 %reshape.186 = bf16[4096,1,320]{2,1,0:T(2,128)(2,1)} reshape(bf16[32,2,20480]{2,1,0:T(2,128)(2,1)} %all-to-all-done.2) | data formatting | bytes 5242880
  310.0 3.3 copy.85
  316.6 4.2 copy.78
  320.8 19.8 %reshape.184 = bf16[4096,1,320]{2,1,0:T(2,128)(2,1)} reshape(bf16[32,2,20480]{2,1,0:T(2,128)(2,1)} %all-to-all-done.1) | data formatting | bytes 5242880
  340.6 3.3 copy.84
  347.2 4.3 copy.74
  351.5 19.8 %reshape.182 = bf16[4096,1,320]{2,1,0:T(2,128)(2,1)} reshape(bf16[32,2,20480]{2,1,0:T(2,128)(2,1)} %all-to-all-done) | data formatting | bytes 5242880
  371.3 3.3 copy.83
  377.9 4.4 copy.71
  384.9 321.9 %while.13 = (s32[]{:T(128)}, bf16[20,8,64,128]{3,2,1,0:T(8,128)(2,1)}, s32[20]{0:T(128)S(1)}, bf16[160,64,128]{2,1,0:T(8,128)(2,1)}, bf16[10368,128]{1,0:T(8,128...) while((s32[]{:T(128)}, ...), condition=%wide.region_3.4_spmd.clone, body=%wide.region_0.3_spmd.clone.sunk | while | flops 136218192 | bytes 15348233 | solution.py:132
  735.7 70.1 %all_to_all.50 = bf16[32,1,320,128]{3,2,1,0:T(8,128)(2,1)S(1)} all-to-all(bf16[32,1,320,128]{3,2,1,0:T(8,128)(2,1)S(1)} %fusion.39), channel_id=1, replica_groups=mesh['section'=8,'seq'=32] {'seq'}, dimensions={0} | all-to-all | bytes 5242880 | tf_op jit(solution)/shard_map/all_to_all | solution.py:18
  806.3 32.3 %collective-permute-done = bf16[1,320,4096]{2,1,0:T(8,128)(2,1)S(1)} collective-permute-done((bf16[1,320,4096]{2,1,0:T(8,128)(2,1)S(1)}, bf16[1,320,4096]{2,1,0:T(8,128)(2,1)S(1)}, u32[]{:S(2)}, u32[]{:S(2)}) %collective-permute-start) | collective-permute-done | bytes 2621472 | tf_op jit(solution)/shard_map/ppermute | solution.py:32
  (486 shorter events, 340.2 us)
Async XLA Ops:
  86.2 11.7 %copy-start.2 = (bf16[1,320,4096]{2,1,0:T(8,128)(2,1)S(1)}, bf16[1,320,4096]{2,1,0:T(8,128)(2,1)}, u32[]{:S(2)}) copy-start(bf16[1,320,4096]{2,1,0:T(8,128)(2,1)} %param.11) | copy-start | bytes 7864324
  86.2 95.3 %all-to-all-start.2 = ((bf16[32,2,20480]{2,1,0:T(2,128)(2,1)}), bf16[32,2,20480]{2,1,0:T(2,128)(2,1)}, u32[]{:S(2)}, u32[]{:S(2)}) async-start(bf16[32,2,20480]{2,1,0:T(2,128)(2,1)} %reshape.185), calls=%async_computation.2 | async-start | bytes 5242880 | tf_op jit(solution)/shard_map/all_to_all | solution.py:142
  181.5 10.1 %copy-start.3 = (bf16[1,320,4096]{2,1,0:T(8,128)(2,1)S(1)}, bf16[1,320,4096]{2,1,0:T(8,128)(2,1)}, u32[]{:S(2)}) copy-start(bf16[1,320,4096]{2,1,0:T(8,128)(2,1)} %param.10) | copy-start | bytes 7864324
  181.5 93.8 %all-to-all-start.1 = ((bf16[32,2,20480]{2,1,0:T(2,128)(2,1)}), bf16[32,2,20480]{2,1,0:T(2,128)(2,1)}, u32[]{:S(2)}, u32[]{:S(2)}) async-start(bf16[32,2,20480]{2,1,0:T(2,128)(2,1)} %reshape.183), calls=%async_computation.1 | async-start | bytes 5242880 | tf_op jit(solution)/shard_map/all_to_all | solution.py:141
  275.3 10.0 %copy-start.5 = (s32[1,2]{1,0:T(1,128)S(1)}, s32[1,2]{1,0:T(1,128)}, u32[]{:S(2)}) copy-start(s32[1,2]{1,0:T(1,128)} %param.16) | copy-start | bytes 28
  275.3 12.4 %copy-start.4 = (s32[1,160,3]{1,0,2:T(1,128)S(1)}, s32[1,160,3]{1,0,2:T(1,128)}, u32[]{:S(2)}) copy-start(s32[1,160,3]{1,0,2:T(1,128)} %param.17) | copy-start | bytes 5764
  275.3 76.2 %all-to-all-start = ((bf16[32,2,20480]{2,1,0:T(2,128)(2,1)}), bf16[32,2,20480]{2,1,0:T(2,128)(2,1)}, u32[]{:S(2)}, u32[]{:S(2)}) async-start(bf16[32,2,20480]{2,1,0:T(2,128)(2,1)} %reshape.181), calls=%async_computation | async-start | bytes 5242880 | tf_op jit(solution)/shard_map/all_to_all | solution.py:139
  377.9 4.4 copy-start
  377.9 4.4 copy-start.1
  806.2 32.3 %collective-permute-start = (bf16[1,320,4096]{2,1,0:T(8,128)(2,1)S(1)}, bf16[1,320,4096]{2,1,0:T(8,128)(2,1)S(1)}, u32[]{:S(2)}, u32[]{:S(2)}) collective-permute-start(bf16[1,320,4096]{2,1,0:T(8,128)(2,1)S(1)} %copy_bitcast_fusion), channel_id=1, source_target_pairs={{0,32},{32,64},{64,96},{96,128},{128,160},{160,192},{192,224},{224... | collective-permute-start | bytes 7864328 | tf_op jit(solution)/shard_map/ppermute | solution.py:32
